TPU v7x, 32 devices: a whole 2x2x4 slice. The times are simulated.
32 devices in a mesh: groups: 2 (over y), ctx: 16 (over z, x, core).
Axes of the slice: x: 2, y: 2, z: 4, core: 2. Of those that a mesh axis runs over, the one named last changes fastest.
Arguments:
- hidden: bfloat16 [4, 4, 8192], P(None, 'groups', 'ctx'), parts along dimension 1, may hold values from -6 to 6
- norm_gain: bfloat16 [8192], P('ctx'), may hold values from 0.5 to 1.5
- w_query: bfloat16 [8192, 8192], P('ctx')
- w_key: bfloat16 [8192, 1024], P('ctx'), may hold values from -0.25 to 0.25
- w_value: bfloat16 [8192, 1024], P('ctx'), may hold values from -0.125 to 0.125
- w_output: bfloat16 [8192, 8192], P('ctx'), may hold values from -0.09375 to 0.09375
- key_cache: bfloat16 [512, 128, 8, 128], P(('groups', 'ctx')), parts along dimension 0, may hold values from -6 to 6
- value_cache: bfloat16 [512, 128, 8, 128], P(('groups', 'ctx')), parts along dimension 0, may hold values from -6 to 6
- retrieval: int32 [8], replicated, may hold values from 0 to 1, as said below
- page_table: int32 [4, 128], P('groups'), parts along dimension 0, may hold values from 0 to 255, as said below
- lengths: int32 [4], P('groups'), parts along dimension 0, may hold values from 4096 to 16384, as said below
- window_start: int32 [4], P('groups'), parts along dimension 0, may hold values from 2945 to 15360, as said below
Outputs:
- attention_out: bfloat16 [4, 4, 8192], P(None, 'groups', 'ctx'), parts along dimension 1
There are 2 independent parts, one for each index of `groups`. A program takes and returns all parts, laid end to end along the dimension named above; an argument that names none is the same for every part. Nothing has to cross between parts.
Inputs may be any that keep to these rules, and one draw needn't show every extreme that they name: `retrieval`: at least one key/value head of each kind. `page_table`: every page number appears exactly once; page g is row g of key_cache and value_cache. `lengths`: some request has exactly 16384 cached positions. lengths[b] - 1152 < window_start[b] <= lengths[b] - 1024.
All inputs are finite; a program needn't handle non-finite values.
Results may differ from a plain program's by a relative error of at most 0.0034.
The roundings to bfloat16 on the way count: a program that leaves them out, or rounds other values in their place, can miss the bound.
Values sent between devices are 32-bit elements; how exact they have to be, the bound alone decides.
A program may use at most 128 MiB of HBM per device.

v0:
```python
import jax
import jax.numpy as jnp
from jax import lax
from jax.sharding import PartitionSpec as P

D = 8192
SINKS = 4


very_low = -1e30
epsilon = 1e-05


def merged_2(shard, axis, combine):
    everything = jax.tree.map(lambda part: lax.all_gather(part, axis), shard)
    first = jax.tree.map(lambda part: part[0], everything)

    def turn(k, so_far):
        return combine(so_far, jax.tree.map(lambda part: part[k], everything))

    return lax.fori_loop(1, lax.axis_size(axis), turn, first)


def combine(earlier, later):
    top_a, total_a, summed_a = earlier
    top_b, total_b, summed_b = later
    highest = jnp.maximum(top_a, top_b)
    factor_a = jnp.exp(top_a - highest)
    factor_b = jnp.exp(top_b - highest)
    return (
        highest,
        total_a * factor_a + total_b * factor_b,
        summed_a * factor_a[..., None] + summed_b * factor_b[..., None],
    )


def arrange(top_val, total_val, summed_val, row_count):
    head_count = top_val.shape[1] * top_val.shape[2]
    top_val = jnp.transpose(top_val, (3, 0, 1, 2)).reshape(row_count, head_count)
    total_val = jnp.transpose(total_val, (3, 0, 1, 2)).reshape(row_count, head_count)
    summed_val = jnp.transpose(summed_val, (3, 0, 1, 2, 4)).reshape(
        row_count, head_count, summed_val.shape[-1]
    )
    return (top_val, total_val, summed_val)


def page_partials(
    query_heads, page_keys, page_values, retrieval, page_table, lengths, window_start, first_page
):
    page_count, page_len, kv_heads, head_dim = page_keys.shape
    batch_size, blocks = page_table.shape
    steps_n = query_heads.shape[0]
    slot_ids = first_page + jnp.arange(page_count, dtype=jnp.int32)
    matches = (page_table[None, :, :] == slot_ids[:, None, None]).astype(jnp.int32)
    owner_req = jnp.sum(
        matches * jnp.arange(batch_size, dtype=jnp.int32)[None, :, None], axis=(1, 2)
    )
    block_ids = jnp.sum(matches * jnp.arange(blocks, dtype=jnp.int32)[None, None, :], axis=(1, 2))
    query_page = query_heads[:, owner_req]
    scores = jnp.einsum(
        "spkgd,ptkd->pkgst", query_page, page_keys, preferred_element_type=jnp.float32
    ) * head_dim ** (-0.5)
    positions = block_ids[:, None] * page_len + jnp.arange(page_len, dtype=jnp.int32)[None, :]
    in_range = positions < lengths[owner_req][:, None]
    recent = (positions < SINKS) | (positions >= window_start[owner_req][:, None])
    visible = in_range[:, None, :] & ((retrieval[None, :, None] == 1) | recent[:, None, :])
    visible = visible[:, :, None, None, :]
    masked = jnp.where(visible, scores, very_low)
    owner_hot = owner_req[:, None] == jnp.arange(batch_size, dtype=jnp.int32)[None, :]
    page_max = jnp.max(masked, axis=-1)
    local_max = jnp.max(
        jnp.where(owner_hot[:, :, None, None, None], page_max[:, None], very_low), axis=0
    )
    row_max = local_max[owner_req]
    weights = jnp.where(visible, jnp.exp(masked - row_max[..., None]), 0.0)
    owner_float = owner_hot.astype(jnp.float32)
    local_total = jnp.einsum(
        "pb,pkgs->bkgs", owner_float, jnp.sum(weights, axis=-1), precision=lax.Precision.HIGHEST
    )
    values = jnp.einsum(
        "pkgst,ptkd->pkgsd",
        weights.astype(jnp.bfloat16),
        page_values,
        preferred_element_type=jnp.float32,
    )
    local_sum = jnp.einsum("pb,pkgsd->bkgsd", owner_float, values, precision=lax.Precision.HIGHEST)
    return arrange(local_max, local_total, local_sum, steps_n * batch_size)


def fresh_partials(query_heads, key_heads, value_heads):
    steps_n, batch_size, kv_heads, group, head_dim = query_heads.shape
    scores = jnp.einsum(
        "sbkgd,ubkd->bkgsu", query_heads, key_heads, preferred_element_type=jnp.float32
    ) * head_dim ** (-0.5)
    causal = jnp.arange(steps_n)[:, None] >= jnp.arange(steps_n)[None, :]
    masked = jnp.where(causal, scores, very_low)
    highest = jnp.max(masked, axis=-1)
    weights = jnp.where(causal, jnp.exp(masked - highest[..., None]), 0.0)
    totals = jnp.sum(weights, axis=-1)
    summed = jnp.einsum(
        "bkgsu,ubkd->bkgsd",
        weights.astype(jnp.bfloat16),
        value_heads,
        preferred_element_type=jnp.float32,
    )
    return arrange(highest, totals, summed, steps_n * batch_size)


def local(
    hidden,
    norm_gain,
    w_query,
    w_key,
    w_value,
    w_output,
    key_cache,
    value_cache,
    retrieval,
    page_table,
    lengths,
    window_start,
):
    steps_n, batch_size, width_local = hidden.shape
    row_count = steps_n * batch_size
    page_count, page_len, kv_heads, head_dim = key_cache.shape
    query_width = w_query.shape[1]
    head_count = query_width // head_dim
    floated = hidden.astype(jnp.float32)
    squares = jnp.sum(floated * floated, axis=-1).reshape(row_count, 1)
    normed = (
        (floated * norm_gain.astype(jnp.float32))
        .astype(jnp.bfloat16)
        .reshape(row_count, width_local)
    )
    query_part = jnp.dot(normed, w_query, preferred_element_type=jnp.float32)
    key_part = jnp.dot(normed, w_key, preferred_element_type=jnp.float32)
    value_part = jnp.dot(normed, w_value, preferred_element_type=jnp.float32)
    query_sum, key_sum, value_sum, square_sum = lax.psum(
        (query_part, key_part, value_part, squares), "ctx"
    )
    inv_rms = lax.rsqrt(square_sum / D + epsilon)
    query_heads = (
        (query_sum * inv_rms)
        .astype(jnp.bfloat16)
        .reshape(steps_n, batch_size, kv_heads, head_count // kv_heads, head_dim)
    )
    key_heads = (
        (key_sum * inv_rms).astype(jnp.bfloat16).reshape(steps_n, batch_size, kv_heads, head_dim)
    )
    value_heads = (
        (value_sum * inv_rms).astype(jnp.bfloat16).reshape(steps_n, batch_size, kv_heads, head_dim)
    )
    device = lax.axis_index("ctx")
    local_parts = page_partials(
        query_heads,
        key_cache,
        value_cache,
        retrieval,
        page_table,
        lengths,
        window_start,
        device * page_count,
    )
    fresh_parts = fresh_partials(query_heads, key_heads, value_heads)
    col_share = query_width // lax.axis_size("ctx")
    col_start = device * col_share
    merged = merged_2(local_parts, "ctx", combine)
    highest, totals, summed = combine(merged, fresh_parts)
    attended_full = (
        (summed / totals[..., None]).reshape(row_count, query_width).astype(jnp.bfloat16)
    )
    attended = lax.dynamic_slice_in_dim(attended_full, col_start, col_share, 1)
    partial_out = jnp.dot(attended, w_output, preferred_element_type=jnp.float32)
    reduced = lax.psum_scatter(partial_out, "ctx", scatter_dimension=1, tiled=True)
    return reduced.reshape(steps_n, batch_size, -1).astype(jnp.bfloat16)


def solution(mesh):
    placed = (
        P(None, "groups", "ctx"),
        P("ctx"),
        P("ctx", None),
        P("ctx", None),
        P("ctx", None),
        P("ctx", None),
        P(("groups", "ctx"), None, None, None),
        P(("groups", "ctx"), None, None, None),
        P(),
        P("groups", None),
        P("groups"),
        P("groups"),
    )
    return jax.shard_map(
        local, mesh=mesh, in_specs=placed, out_specs=P(None, "groups", "ctx"), check_vma=False
    )
```

profile of v0, /device:TPU:0, one launch (start us, length us, event | category | flops | bytes accessed | tf_op | source)
XLA Modules:
  0.0 352.0 jit_solution(1187054879857907427)
XLA Ops:
  9.5 2.1 fusion.65
  11.7 5.3 %fusion.63 = f32[8,8192]{1,0:T(8,128)} fusion(bf16[8,512]{1,0:T(8,128)(2,1)S(1)} %reshape.142, bf16[512,8192]{1,0:T(8,128)(2,1)} %param.16), kind=kOutput, calls=%fused_computation.100 | convolution fusion | flops 67108864 | bytes 8658944 | tf_op jit(solution)/shard_map/dot_general | solution.py:135
  19.2 2.5 compare_select_fusion.4
  21.9 77.6 %all-reduce.6.cloned.1.call-done = (f32[8,1]{0,1:T(1,128)}, f32[8,1024]{1,0:T(8,128)}, f32[8,1024]{1,0:T(8,128)}) async-done(((f32[8,1]{0,1:T(1,128)}, f32[8,1024]{1,0:T(8,128)}, f32[8,1024]{1,0:T(8,128)}), (f32[8,1]{0,1:T(1,128)}, f32[8,1024]{1,0:T(8,128)}, f32[8,1024]{1,0:T(8,128)})) %all-reduce.6.cloned.1.call-update) | async-done | bytes 65584 | tf_op jit(solution)/shard_map/psum | solution.py:138
  100.1 93.8 %all-reduce.4.cloned.1.call-done = f32[8,8192]{1,0:T(8,128)} async-done(((f32[8,8192]{1,0:T(8,128)}), f32[8,8192]{1,0:T(8,128)}) %all-reduce.4.cloned.1.call-update) | async-done | bytes 262160 | tf_op jit(solution)/shard_map/psum | solution.py:138
  195.0 1.6 gather_fusion
  196.7 5.0 %bitcast_reduce_fusion = (f32[16,8,8,4]{2,3,1,0:T(4,128)S(1)}, f32[16,8,4,8,128]{4,3,2,1,0:T(8,128)S(1)}) fusion(pred[16,8,128]{2,1,0:T(8,128)(4,1)S(1)} %or_and_fusion, bf16[16,128,8,128,1]{3,2,1,0,4:T(8,128)(2,1)} %bitcast.124, bf16[16,4,8,8,128]{4,3,2,1,0:T(8,128)(2,1)} %gather_fusion), kind=kOutput, calls=%fused_computation.15 | convolution fusion | flops 135786496 | bytes 7372800 | tf_op jit(solution)/shard_map/spkgd,ptkd->pkgst/dot_general | solution.py:60
  204.1 1.4 gather_fusion.1
  206.5 3.6 %fusion.3 = f32[16,8,8,4,128]{4,2,3,1,0:T(8,128)S(1)} fusion(bf16[16,128,8,128,1]{3,2,1,0,4:T(8,128)(2,1)} %bitcast.133, f32[16,8,4,8,128]{4,3,2,1,0:T(8,128)S(1)} %get-tuple-element.227, f32[16,8,8,4]{2,3,1,0:T(4,128)S(1)} %copy.83, pred[16,8,128]{2,1,0:T(8,128)(4,1)S(1)} %or_and_fusion), kind=kOutput, calls=%fused_computation.10 | convolution fusion | flops 136839168 | bytes 8421376 | tf_op jit(solution)/shard_map/pkgst,ptkd->pkgsd/dot_general | solution.py:80
  210.1 2.0 fusion.9
  216.6 1.4 reshape.149
  218.0 1.4 copy.81
  219.4 1.4 all_gather_reshape.9
  220.8 1.4 fusion.12
  224.6 21.5 %all_gather.9 = f32[16,8,64]{2,1,0:T(8,128)S(1)} all-gather(f32[1,8,64]{2,1,0:T(8,128)} %all_gather_reshape.9), channel_id=1, replica_groups=mesh['groups'=2,'ctx'=16] {'ctx'}, dimensions={0}, use_global_device_ids=true | all-gather | bytes 34816 | tf_op jit(solution)/shard_map/all_gather | solution.py:15
  246.1 17.9 %all_gather.10 = f32[16,8,64]{2,1,0:T(8,128)S(1)} all-gather(f32[1,8,64]{2,1,0:T(8,128)S(1)} %all_gather_reshape.10), channel_id=1, replica_groups=mesh['groups'=2,'ctx'=16] {'ctx'}, dimensions={0}, use_global_device_ids=true | all-gather | bytes 34816 | tf_op jit(solution)/shard_map/all_gather | solution.py:15
  265.5 18.9 %while.19 = (s32[]{:T(128)}, f32[8,64]{1,0:T(8,128)S(1)}, f32[8,64]{1,0:T(8,128)S(1)}, f32[8,64,128]{2,1,0:T(8,128)S(1)}, f32[16,8,64]{2,1,0:T(8,128)S(1)}, /*in...) while((s32[]{:T(128)}, f32[8,64]{1,0:T(8,128)S(1)}, ...), condition=%wide.region_9.10_spmd, body=%wide.region_8.9_spmd.sunk | while | flops 199685 | bytes 807063 | solution.py:21
  265.5 1.2 fusion.77
  266.8 1.2 fusion.77
  269.3 1.2 fusion.77
  270.6 1.2 fusion.77
  271.8 1.2 fusion.77
  284.8 5.3 %fusion.41 = f32[8,8192]{1,0:T(8,128)} fusion(bf16[512,8192]{1,0:T(8,128)(2,1)} %param.19, bf16[8,8192]{1,0:T(8,128)(2,1)S(1)} %bitcast.129, s32[]{:T(128)S(6)} %select_n.56), kind=kOutput, calls=%fused_computation.65 | convolution fusion | flops 67108864 | bytes 8658948 | tf_op jit(solution)/shard_map/dot_general | solution.py:173
  290.1 54.1 %reduce-scatter.2.cloned.1.call-done = f32[8,512]{1,0:T(8,128)} async-done(((f32[8,8192]{1,0:T(8,128)}), f32[8,512]{1,0:T(8,128)}) %reduce-scatter.2.cloned.1.call-update) | async-done | bytes 16400 | tf_op jit(solution)/shard_map/reduce_scatter | solution.py:174
  (111 shorter events, 32.9 us)
Async XLA Ops:
  6.5 2.1 copy-start
  6.5 93.0 %all-reduce.6.cloned.1.call-start = ((), (), s32[]{:S(2)}) async-start(), calls=%async_computation.4 | async-start | bytes 132096 | tf_op jit(solution)/shard_map/psum | solution.py:138
  11.6 5.5 %copy-start.14 = (s32[2,128]{1,0:T(2,128)S(1)}, s32[2,128]{1,0:T(2,128)}, u32[]{:S(2)}) copy-start(s32[2,128]{1,0:T(2,128)} %param.23) | copy-start | bytes 3076
  11.6 6.3 %copy-start.11 = (s32[2]{0:T(128)S(1)}, s32[2]{0:T(128)}, u32[]{:S(2)}) copy-start(s32[2]{0:T(128)} %param.24) | copy-start | bytes 28
  11.7 6.9 %copy-start.12 = (s32[2]{0:T(128)S(1)}, s32[2]{0:T(128)}, u32[]{:S(2)}) copy-start(s32[2]{0:T(128)} %param.25) | copy-start | bytes 28
  11.7 7.5 %copy-start.15 = (s32[8]{0:T(128)S(1)}, s32[8]{0:T(128)}, u32[]{:S(2)}) copy-start(s32[8]{0:T(128)} %param.22) | copy-start | bytes 100
  11.7 182.3 %all-reduce.4.cloned.1.call-start = ((), (), s32[]{:S(2)}) async-start(), calls=%async_computation.1 | async-start | bytes 524288 | tf_op jit(solution)/shard_map/psum | solution.py:138
  17.0 247.5 %all-gather.2.cloned.1.call-start = ((), (), s32[]{:S(2)}) async-start(), calls=%async_computation.2 | async-start | bytes 4456448 | tf_op jit(solution)/shard_map/all_gather | solution.py:15
  17.3 4.5 %copy-start.6 = (s32[16]{0:T(128)}, s32[16]{0:T(128)S(1)}, u32[]{:S(2)}) copy-start(s32[16]{0:T(128)S(1)} %get-tuple-element.187) | copy-start | bytes 196
  19.2 177.4 %copy-start.9 = (s32[1024]{0:T(1024)}, s32[1024]{0:T(1024)S(1)}, u32[]{:S(2)}) copy-start(s32[1024]{0:T(1024)S(1)} %pad_clamp_fusion) | copy-start | bytes 12292
  100.1 96.5 %copy-start.10 = (f32[8]{0:T(128)}, f32[8]{0:T(128)S(1)}, u32[]{:S(2)}) copy-start(f32[8]{0:T(128)S(1)} %rsqrt_bitcast_fusion) | copy-start | bytes 100
  203.5 0.6 copy-start.3
  206.5 3.6 %copy-start.7 = (s32[16]{0:T(128)S(1)}, s32[16]{0:T(128)}, u32[]{:S(2)}) copy-start(s32[16]{0:T(128)} %copy-done.6) | copy-start | bytes 196
  212.9 131.3 %reduce-scatter.2.cloned.1.call-start = ((), (), s32[]{:S(2)}) async-start(), calls=%async_computation.3 | async-start | bytes 278528 | tf_op jit(solution)/shard_map/reduce_scatter | solution.py:174
  212.9 3.0 copy-start.13
  215.1 0.7 copy-start.1
  215.1 0.8 copy-start.4
  215.9 7.6 %copy-start.2 = (f32[2,8,8,4,4]{2,4,3,1,0:T(4,128)S(1)}, f32[2,8,8,4,4]{2,4,3,1,0:T(4,128)}, u32[]{:S(2)}) copy-start(f32[2,8,8,4,4]{2,4,3,1,0:T(4,128)} %copy-done.1) | copy-start | bytes 24580
  220.8 1.4 copy-start.8
  265.5 18.9 %copy-start.5 = (f32[8,64]{1,0:T(8,128)S(1)}, f32[8,64]{1,0:T(8,128)}, u32[]{:S(2)}) copy-start(f32[8,64]{1,0:T(8,128)} %reshape.149) | copy-start | bytes 6148
Sparse Core Ops, SparseCore 0:
  11.8 87.7 all-reduce.5
  103.3 90.6 all-reduce.3
  213.0 51.4 all-gather.1
  290.2 53.9 reduce-scatter.1
where the time goes:
time: 353 us; the launch traced here: 352 us
  waiting for transfers between devices  226 us (64%)
  blocking collectives  39.4 us (11%)
  other arithmetic  29.6 us (8%)
  matrix products  26.1 us (7%)
  local copies, waits for them, and re-layouts  16.8 us (5%)
  between operations  13.5 us (4%)
    psum x2, waiting for transfers between devices, local(): lax.psum((query_part, key_part, value_part, squares), 'ctx')  171 us
    reduce_scatter x1, waiting for transfers between devices, local(): lax.psum_scatter(partial_out, 'ctx', scatter_dimension=1, tiled=True)  54.1 us
    all_gather x2, blocking collectives, merged_2(): everything = jax.tree.map(lambda part: lax.all_gather(part, axis), shard)  39.4 us
    add x15, other arithmetic, combine(): summed_a * factor_a[..., None] + summed_b * factor_b[..., None]  18.2 us
  transfers between devices with their start and end apart: 4, of which 4 were waited for; matrix products, arithmetic and copies ran while one was open for 6% of the time, Pallas kernels for 0%

commit v1 on v0

--- a/solution.py
+++ b/solution.py
@@ -1,6 +1,10 @@
+import functools
+
 import jax
 import jax.numpy as jnp
 from jax import lax
+from jax.experimental import pallas as pl
+from jax.experimental.pallas import tpu as pltpu
 from jax.sharding import PartitionSpec as P
 
 D = 8192
@@ -106,7 +110,7 @@
     return arrange(highest, totals, summed, steps_n * batch_size)
 
 
-def local(
+def local_small(
     hidden,
     norm_gain,
     w_query,
@@ -175,6 +179,467 @@
     return reduced.reshape(steps_n, batch_size, -1).astype(jnp.bfloat16)
 
 
+def swap_halves(first, second):
+    low = lax.broadcasted_iota(jnp.int32, first.shape, 0) < first.shape[0] // 2
+    half = first.shape[0] // 2
+    return (
+        jnp.where(low, first, pltpu.roll(second, half, 0)),
+        jnp.where(low, pltpu.roll(first, half, 0), second),
+    )
+
+
+def fused(
+    n,
+    steps_n,
+    batch,
+    kv_heads,
+    page_len,
+    retrieval_ref,
+    lengths_ref,
+    window_ref,
+    hidden_ref,
+    gain_ref,
+    table_ref,
+    wq_hbm,
+    wk_hbm,
+    wv_hbm,
+    wo_hbm,
+    keys_hbm,
+    values_hbm,
+    out_ref,
+    wq_v,
+    wkv_v,
+    wo_v,
+    keys_v,
+    values_v,
+    values_t,
+    msg1,
+    recv1,
+    gath,
+    queries,
+    queries_t,
+    info,
+    page_max,
+    page_total,
+    page_sum,
+    msg3,
+    recv3,
+    msg4,
+    recv4,
+    wq_sem,
+    wo_sem,
+    wkv_sem,
+    keys_sem,
+    values_sem,
+    send_sem,
+    recv_sem,
+):
+    f32, bf16 = jnp.float32, jnp.bfloat16
+    me = lax.axis_index("ctx")
+    pages = keys_v.shape[0]
+    share = wq_v.shape[2]
+    width = share * n
+    dim = 128
+    width_local = hidden_ref.shape[1]
+    scale = dim ** (-0.5)
+
+    def peer(i):
+        return lax.rem(me + i, n)
+
+    def source(i):
+        return lax.rem(me + n - i, n)
+
+    def wq_copy(i):
+        cols = pl.ds(pl.multiple_of(peer(i) * share, 128), share)
+        return pltpu.make_async_copy(wq_hbm.at[:, cols], wq_v.at[i], wq_sem.at[i])
+
+    def wo_copy(i):
+        cols = pl.ds(pl.multiple_of(peer(i) * share, 128), share)
+        return pltpu.make_async_copy(wo_hbm.at[:, cols], wo_v.at[i], wo_sem.at[i])
+
+    kv_width = kv_heads * dim
+    wk_copy = pltpu.make_async_copy(wk_hbm, wkv_v.at[:, pl.ds(0, kv_width)], wkv_sem.at[0])
+    wv_copy = pltpu.make_async_copy(wv_hbm, wkv_v.at[:, pl.ds(kv_width, kv_width)], wkv_sem.at[1])
+
+    def keys_copy(p):
+        return pltpu.make_async_copy(keys_hbm.at[p], keys_v.at[p], keys_sem.at[p])
+
+    def values_copy(p):
+        return pltpu.make_async_copy(values_hbm.at[p], values_v.at[p], values_sem.at[p])
+
+    def remote(phase, i, from_ref, to_ref):
+        return pltpu.make_async_remote_copy(
+            src_ref=from_ref,
+            dst_ref=to_ref,
+            send_sem=send_sem.at[phase, i],
+            recv_sem=recv_sem.at[phase, i],
+            device_id={"ctx": peer(i)},
+            device_id_type=pl.DeviceIdType.MESH,
+        )
+
+    barrier = pltpu.get_barrier_semaphore()
+
+    @pl.loop(1, n)
+    def _(i):
+        pl.semaphore_signal(
+            barrier, inc=1, device_id={"ctx": peer(i)}, device_id_type=pl.DeviceIdType.MESH
+        )
+
+    wk_copy.start()
+    wv_copy.start()
+
+    @pl.loop(1, n + 1)
+    def _(i):
+        wq_copy(lax.rem(i, n)).start()
+
+    @pl.loop(0, pages)
+    def _(p):
+        values_copy(p).start()
+
+    @pl.loop(0, pages)
+    def _(p):
+        keys_copy(p).start()
+
+    @pl.loop(1, n + 1)
+    def _(i):
+        wo_copy(lax.rem(i, n)).start()
+
+    floated = hidden_ref[...].astype(f32)
+    squares = jnp.sum(floated * floated, axis=1, keepdims=True)
+    squares = jnp.broadcast_to(squares, (floated.shape[0], dim))
+    normed = (floated * gain_ref[...].astype(f32)).astype(bf16)
+
+    table = table_ref[...]
+    page_id = lax.broadcasted_iota(jnp.int32, (pages, table.shape[1]), 0) + me * pages
+    lane_block = lax.broadcasted_iota(jnp.int32, (pages, table.shape[1]), 1).astype(f32)
+    owner_of = jnp.zeros((pages, 1), f32)
+    base_of = jnp.zeros((pages, 1), f32)
+    length_of = jnp.zeros((pages, 1), f32)
+    window_of = jnp.zeros((pages, 1), f32)
+    for b in range(batch):
+        hit = jnp.where(table[b : b + 1, :] == page_id, 1.0, 0.0)
+        found = jnp.sum(hit, axis=1, keepdims=True)
+        owner_of += found * float(b)
+        base_of += jnp.sum(hit * lane_block, axis=1, keepdims=True) * float(page_len)
+        length_of += found * lengths_ref[b].astype(f32)
+        window_of += found * window_ref[b].astype(f32)
+    for row, value in enumerate((owner_of, base_of, length_of, window_of)):
+        info[row] = jnp.broadcast_to(value, (pages, dim)).astype(jnp.int32)
+
+    wk_copy.wait()
+    wv_copy.wait()
+    pl.semaphore_wait(barrier, n - 1)
+
+    def project(i, to_ref):
+        wq_copy(i).wait()
+        cols = pl.ds(pl.multiple_of(peer(i) * dim, 128), dim)
+        to_ref[:, pl.ds(0, share)] = jnp.dot(normed, wq_v[i], preferred_element_type=f32)
+        to_ref[:, pl.ds(share, dim)] = jnp.dot(normed, wkv_v[:, cols], preferred_element_type=f32)
+        to_ref[:, pl.ds(share + dim, dim)] = squares
+
+    @pl.loop(1, n)
+    def _(i):
+        project(i, msg1.at[i])
+        remote(0, i, msg1.at[i], recv1.at[me]).start()
+
+    project(0, recv1.at[me])
+
+    @pl.loop(0, pages)
+    def _(p):
+        values_copy(p).wait()
+        values_t[p] = values_v[p].T
+
+    def add_up(phase, msg, recv, acc):
+        def turn(i, acc):
+            remote(phase, i, msg.at[i], recv.at[source(i)]).wait_recv()
+            return acc + recv[source(i)]
+
+        return lax.fori_loop(1, n, turn, acc)
+
+    summed = add_up(0, msg1, recv1, recv1[me])
+    inv_rms = lax.rsqrt(summed[:, share + dim :] / (width_local * n) + epsilon)
+    for c in range((share + dim) // dim):
+        piece = summed[:, c * dim : (c + 1) * dim] * inv_rms
+        gath[me, :, pl.ds(c * dim, dim)] = piece.astype(bf16).astype(f32)
+
+    @pl.loop(1, n)
+    def _(i):
+        remote(1, i, gath.at[me], gath.at[me]).start()
+
+    def spread(j):
+        rows = pl.multiple_of(j * 2 * steps_n * batch, 8)
+        for c in range(2):
+            even = gath[j, :, pl.ds(2 * c * dim, dim)]
+            odd = gath[j, :, pl.ds((2 * c + 1) * dim, dim)]
+            low, high = swap_halves(even, odd)
+            queries[0, pl.ds(rows + 8 * c, 8), :] = low
+            queries[1, pl.ds(rows + 8 * c, 8), :] = high
+
+    spread(me)
+
+    @pl.loop(1, n)
+    def _(i):
+        remote(1, i, gath.at[me], gath.at[source(i)]).wait_recv()
+        spread(source(i))
+
+    q_rows = queries.shape[1]
+    for b in range(batch):
+        queries_t[b] = queries[b].T.astype(bf16)
+
+    sub = lax.broadcasted_iota(jnp.int32, (kv_heads, dim), 0)
+    lane = lax.broadcasted_iota(jnp.int32, (kv_heads, dim), 1)
+    per_head = q_rows // kv_heads
+    lower = sub < kv_heads // 2
+    own_lane = (lane // per_head) == lax.rem(sub, kv_heads // 2)
+    full_head = jnp.zeros((kv_heads, dim), jnp.int32)
+    for k in range(kv_heads):
+        full_head = jnp.where(sub == k, retrieval_ref[k], full_head)
+    full_head = full_head == 1
+
+    @pl.loop(0, pages)
+    def _(p):
+        keys_copy(p).wait()
+        owner = info[0, pl.ds(p, 1), :]
+        base = info[1, pl.ds(p, 1), :]
+        until = jnp.where(own_lane, info[2, pl.ds(p, 1), :], 0) - base
+        since = jnp.where(full_head, 0, info[3, pl.ds(p, 1), :]) - base
+        sinks = SINKS - jnp.broadcast_to(base, (kv_heads, dim))
+        wide_owner = jnp.concatenate([owner, owner], axis=1)
+        query = jnp.where(
+            wide_owner == 1, queries_t[1].astype(f32), queries_t[0].astype(f32)
+        ).astype(bf16)
+        scores = jnp.dot(keys_v[p], query, preferred_element_type=f32)
+        scores = scores.reshape(page_len, kv_heads, q_rows)
+        merged = jnp.where(lower[None], scores[:, :, :dim], scores[:, :, dim:]) * scale
+        token = lax.broadcasted_iota(jnp.int32, (page_len, kv_heads, dim), 0)
+        visible = (token < until[None]) & ((token >= since[None]) | (token < sinks[None]))
+        masked = jnp.where(visible, merged, very_low)
+        highest = jnp.max(masked, axis=0)
+        weights = jnp.where(visible, jnp.exp(masked - highest[None]), 0.0)
+        page_max[p] = highest
+        page_total[p] = jnp.sum(weights, axis=0)
+        wide = jnp.concatenate(
+            [jnp.where(lower[None], weights, 0.0), jnp.where(lower[None], 0.0, weights)], axis=2
+        )
+        wide = wide.reshape(page_len * kv_heads, q_rows).astype(bf16)
+        page_sum[p] = jnp.dot(values_t[p], wide, preferred_element_type=f32)
+
+    def lanes_of(stat):
+        kept = jnp.where(own_lane, stat, 0.0)
+        return jnp.concatenate(
+            [
+                jnp.sum(jnp.where(lower, kept, 0.0), axis=0, keepdims=True),
+                jnp.sum(jnp.where(lower, 0.0, kept), axis=0, keepdims=True),
+            ],
+            axis=1,
+        )
+
+    def top_turn(p, tops):
+        owner = info[0, pl.ds(p, 1), :]
+        return tuple(
+            jnp.where(owner == b, jnp.maximum(top, page_max[p]), top) for b, top in enumerate(tops)
+        )
+
+    start = jnp.full((kv_heads, dim), very_low, f32)
+    tops = lax.fori_loop(0, pages, top_turn, (start,) * batch)
+
+    def sum_turn(p, totals):
+        owner = info[0, pl.ds(p, 1), :]
+        top = jnp.where(owner == 1, tops[1], tops[0])
+        factor = jnp.exp(page_max[p] - top)
+        term = factor * page_total[p]
+        totals = tuple(total + jnp.where(owner == b, term, 0.0) for b, total in enumerate(totals))
+        page_sum[p] = page_sum[p] * lanes_of(factor)
+        return totals
+
+    totals = lax.fori_loop(0, pages, sum_turn, (jnp.zeros((kv_heads, dim), f32),) * batch)
+
+    for b in range(batch):
+        acc = jnp.zeros((dim, q_rows), f32)
+        for p in range(pages):
+            owner = info[0, pl.ds(p, 1), :]
+            wide_owner = jnp.concatenate([owner, owner], axis=1)
+            acc += jnp.where(wide_owner == b, page_sum[p], 0.0)
+        msg3[:, pl.ds(16 * b, 16), :] = acc.T.reshape(n, q_rows // n, dim)
+    stats = []
+    for b in range(batch):
+        for stat in (tops[b], totals[b]):
+            stats.append(jnp.broadcast_to(lanes_of(stat), (dim // 4, q_rows)))
+    msg3[:, pl.ds(32, 16), :] = jnp.concatenate(stats, axis=0).T.reshape(n, q_rows // n, dim)
+
+    @pl.loop(1, n)
+    def _(i):
+        remote(2, i, msg3.at[peer(i)], recv3.at[me]).start()
+
+    recv3[me] = msg3[me]
+
+    mine = pl.ds(pl.multiple_of(me * 16, 8), 16)
+    own_query = jnp.concatenate([queries[b, mine, :] for b in range(batch)], axis=0)
+    head = me // 2
+    new_key = gath[head, :, pl.ds(share, dim)]
+    new_value = gath[kv_heads + head, :, pl.ds(share, dim)]
+    fresh = (
+        lax.dot_general(
+            own_query, new_key, (((1,), (1,)), ((), ())), preferred_element_type=f32
+        )
+        * scale
+    )
+    row = lax.broadcasted_iota(jnp.int32, fresh.shape, 0)
+    col = lax.broadcasted_iota(jnp.int32, fresh.shape, 1)
+    causal = (row // 16 == col // steps_n) & (lax.rem(row, steps_n) >= lax.rem(col, steps_n))
+    fresh = jnp.where(causal, fresh, very_low)
+    fresh_max = jnp.max(fresh, axis=1, keepdims=True)
+    fresh_weights = jnp.where(causal, jnp.exp(fresh - fresh_max), 0.0)
+    fresh_total = jnp.sum(fresh_weights, axis=1, keepdims=True)
+    fresh_sum = jnp.dot(
+        fresh_weights.astype(bf16).astype(f32), new_value, preferred_element_type=f32
+    )
+
+    @pl.loop(1, n)
+    def _(i):
+        remote(2, i, msg3.at[peer(i)], recv3.at[source(i)]).wait_recv()
+
+    top = lax.fori_loop(
+        0,
+        n,
+        lambda j, top: jnp.maximum(top, recv3[j, pl.ds(32, 16), :]),
+        jnp.full((16, dim), very_low, f32),
+    )
+    attended = []
+    for b in range(batch):
+        rows = slice(16 * b, 16 * b + 16)
+        highest = jnp.maximum(top[:, 64 * b : 64 * b + 1], fresh_max[rows])
+        factor = jnp.exp(fresh_max[rows] - highest)
+        total = fresh_total[rows] * factor
+        acc = fresh_sum[rows] * factor
+
+        def merge_turn(j, state, b=b, highest=highest):
+            total, acc = state
+            stat = recv3[j, pl.ds(32, 16), :]
+            factor = jnp.exp(stat[:, 64 * b : 64 * b + 1] - highest)
+            total = total + stat[:, 64 * b + 32 : 64 * b + 33] * factor
+            return total, acc + recv3[j, pl.ds(16 * b, 16), :] * factor
+
+        total, acc = lax.fori_loop(0, n, merge_turn, (total, acc))
+        attended.append(acc / total)
+    first = swap_halves(attended[0][:8], attended[1][:8])
+    second = swap_halves(attended[0][8:], attended[1][8:])
+    attended = jnp.concatenate(first + second, axis=1).astype(bf16)
+
+    def project_out(i):
+        wo_copy(i).wait()
+        return jnp.dot(attended, wo_v[i], preferred_element_type=f32)
+
+    @pl.loop(1, n)
+    def _(i):
+        msg4[i] = project_out(i)
+        remote(3, i, msg4.at[i], recv4.at[me]).start()
+
+    out_ref[...] = add_up(3, msg4, recv4, project_out(0))
+
+    @pl.loop(1, n)
+    def _(i):
+        remote(0, i, msg1.at[i], recv1.at[me]).wait_send()
+        remote(1, i, gath.at[me], gath.at[me]).wait_send()
+        remote(2, i, msg3.at[peer(i)], recv3.at[me]).wait_send()
+        remote(3, i, msg4.at[i], recv4.at[me]).wait_send()
+
+
+def local(
+    hidden,
+    norm_gain,
+    w_query,
+    w_key,
+    w_value,
+    w_output,
+    key_cache,
+    value_cache,
+    retrieval,
+    page_table,
+    lengths,
+    window_start,
+):
+    n = lax.axis_size("ctx")
+    steps_n, batch, width_local = hidden.shape
+    pages, page_len, kv_heads, dim = key_cache.shape
+    query_width = w_query.shape[1]
+    share = query_width // n
+    rows = steps_n * batch
+    q_rows = query_width // dim * steps_n
+    if (n, share, rows, batch, kv_heads, dim) != (2 * kv_heads, 4 * dim, 8, 2, 8, 128):
+        return local_small(
+            hidden,
+            norm_gain,
+            w_query,
+            w_key,
+            w_value,
+            w_output,
+            key_cache,
+            value_cache,
+            retrieval,
+            page_table,
+            lengths,
+            window_start,
+        )
+    f32, bf16 = jnp.float32, jnp.bfloat16
+    smem = pl.BlockSpec(memory_space=pltpu.SMEM)
+    vmem = pl.BlockSpec(memory_space=pltpu.VMEM)
+    hbm = pl.BlockSpec(memory_space=pl.ANY)
+    dma = pltpu.SemaphoreType.DMA
+    out = pl.pallas_call(
+        functools.partial(fused, n, steps_n, batch, kv_heads, page_len),
+        out_shape=jax.ShapeDtypeStruct((rows, w_output.shape[1] // n), f32),
+        in_specs=[smem] * 3 + [vmem] * 3 + [hbm] * 6,
+        out_specs=vmem,
+        scratch_shapes=[
+            pltpu.VMEM((n, width_local, share), bf16),
+            pltpu.VMEM((width_local, 2 * kv_heads * dim), bf16),
+            pltpu.VMEM((n, share, w_output.shape[1] // n), bf16),
+            pltpu.VMEM((pages, page_len * kv_heads, dim), bf16),
+            pltpu.VMEM((pages, page_len * kv_heads, dim), bf16),
+            pltpu.VMEM((pages, dim, page_len * kv_heads), bf16),
+            pltpu.VMEM((n, rows, share + 2 * dim), f32),
+            pltpu.VMEM((n, rows, share + 2 * dim), f32),
+            pltpu.VMEM((n, rows, share + dim), f32),
+            pltpu.VMEM((batch, q_rows, dim), f32),
+            pltpu.VMEM((batch, dim, q_rows), bf16),
+            pltpu.VMEM((4, pages, dim), jnp.int32),
+            pltpu.VMEM((pages, kv_heads, dim), f32),
+            pltpu.VMEM((pages, kv_heads, dim), f32),
+            pltpu.VMEM((pages, dim, q_rows), f32),
+            pltpu.VMEM((n, 48, dim), f32),
+            pltpu.VMEM((n, 48, dim), f32),
+            pltpu.VMEM((n, rows, share), f32),
+            pltpu.VMEM((n, rows, share), f32),
+            dma((n,)),
+            dma((n,)),
+            dma((2,)),
+            dma((pages,)),
+            dma((pages,)),
+            dma((4, n)),
+            dma((4, n)),
+        ],
+        compiler_params=pltpu.CompilerParams(
+            collective_id=0, has_side_effects=True, vmem_limit_bytes=56 * 2**20
+        ),
+    )(
+        retrieval,
+        lengths,
+        window_start,
+        jnp.transpose(hidden, (1, 0, 2)).reshape(rows, width_local),
+        norm_gain.reshape(1, width_local),
+        page_table,
+        w_query,
+        w_key,
+        w_value,
+        w_output,
+        key_cache.reshape(pages, page_len * kv_heads, dim),
+        value_cache.reshape(pages, page_len * kv_heads, dim),
+    )
+    out = out.reshape(batch, steps_n, out.shape[1])
+    return jnp.transpose(out, (1, 0, 2)).astype(bf16)
+
+
 def solution(mesh):
     placed = (
         P(None, "groups", "ctx"),

time: 353 us -> 66 us (0.19)
  waiting for transfers between devices: 226 us -> 0 us
  Pallas kernels: 0 us -> 61.7 us
  blocking collectives: 39.4 us -> 0 us
  other arithmetic: 29.6 us -> 0.72 us
  matrix products: 26.1 us -> 0 us
  local copies, waits for them, and re-layouts: 16.8 us -> 3.2 us
  between operations: 13.5 us -> 0.01 us
    psum x2 -> x0, waiting for transfers between devices: 171 us -> none  [local(): lax.psum((query_part, key_part, value_part, squares), 'ctx')]
    pallas_call x0 -> x1, Pallas kernels: none -> 61.7 us  [local(): pl.pallas_call(functools.partial(fused, n, steps_n, batch, kv_heads, page...]
    reduce_scatter x1 -> x0, waiting for transfers between devices: 54.1 us -> none  [local(): lax.psum_scatter(partial_out, 'ctx', scatter_dimension=1, tiled=True)]
    all_gather x2 -> x0, blocking collectives: 39.4 us -> none  [merged_2(): everything = jax.tree.map(lambda part: lax.all_gather(part, axis), shard)]
    dot_general x10 -> x0, matrix products: 26.1 us -> none  [the longest x1 5.28 us: local(): jnp.dot(attended, w_output, preferred_element_type=jnp.float32)]
    add x32 -> x0, other arithmetic: 18.5 us -> none  [the longest x15 18.2 us: combine(): summed_a * factor_a[..., None] + summed_b * factor_b[..., None]]
    gather x5 -> x0, local copies, waits for them, and re-layouts: 5.32 us -> none  [the longest x2 2.4 us: page_partials(): row_max = local_max[owner_req]]
  transfers between devices with their start and end apart: 4 -> 0, of which waited for: 4 -> 0; matrix products, arithmetic and copies ran while one was open for 6% -> 0% of each run, Pallas kernels for 0% -> 0%
where the time goes in v1:
time: 66 us; the launch traced here: 65.6 us
  Pallas kernels  61.7 us (93%)
  local copies, waits for them, and re-layouts  3.2 us (5%)
  other arithmetic  0.72 us (1%)
    pallas_call x1, Pallas kernels, local(): pl.pallas_call(functools.partial(fused, n, steps_n, batch, kv_heads, page...  61.7 us

profile of v1, /device:TPU:0, one launch (start us, length us, event | category | flops | bytes accessed | tf_op | source)
XLA Modules:
  0.0 65.6 jit_solution(5003001232825387741)
XLA Ops:
  0.0 1.3 %reshape.15.gain_ref = bf16[1,512]{1,0:T(2,128)(2,1)} reshape(bf16[512]{0:T(512)(128)(2,1)} %param.13) | data formatting | bytes 2048 | tf_op jit(solution)/shard_map/reshape | solution.py:630
  1.3 0.7 %copy.13 = bf16[2,4,512]{2,1,0:T(4,128)(2,1)S(1)} copy(bf16[2,4,512]{2,0,1:T(2,128)(2,1)} %bitcast.8) | data formatting | bytes 16384 | tf_op jit(solution)/shard_map/transpose | solution.py:629
  2.0 0.6 reshape.14.hidden_ref
  2.6 61.7 %shard_map.118 = f32[8,512]{1,0:T(8,128)} custom-call(s32[8]{0:T(128)} %retrieval_ref.1, s32[2]{0:T(128)} %lengths_ref.1, s32[2]{0:T(128)} %window_ref.1, bf16[8,512]{1,0:T(8,128)(2,1)} %reshape.14.hidden_ref, bf16[1,512]{1,0:T(2,128)(2,1)} %reshape.15.gain_ref, s32[2,128]{1,0:T(2,128)} %table_ref.1, bf16[512,8192]{1,0:T(8,128)(2,1)} %wq_hbm.1, ...), custom_call_target="tpu_custom_call" | custom-call | tf_op jit(solution)/shard_map/pallas_call | solution.py:589
  64.3 0.7 %convert_element_type.9 = bf16[8,512]{1,0:T(8,128)(2,1)S(1)} convert(f32[8,512]{1,0:T(8,128)} %shard_map.118) | non-fusion elementwise | flops 4096 | bytes 24576 | tf_op jit(solution)/shard_map/convert_element_type | solution.py:640
  65.0 0.6 copy.16
  (1 shorter events, 0.0 us)

commit v2 on v1

--- a/solution.py
+++ b/solution.py
@@ -219,6 +219,7 @@
     queries,
     queries_t,
     info,
+    owners,
     page_max,
     page_total,
     page_sum,
@@ -240,7 +241,7 @@
     share = wq_v.shape[2]
     width = share * n
     dim = 128
-    width_local = hidden_ref.shape[1]
+    width_local = hidden_ref.shape[2]
     scale = dim ** (-0.5)
 
     def peer(i):
@@ -304,10 +305,13 @@
     def _(i):
         wo_copy(lax.rem(i, n)).start()
 
-    floated = hidden_ref[...].astype(f32)
+    loaded = hidden_ref[...].astype(f32)
+    floated = jnp.concatenate(
+        [loaded[s, b : b + 1, :] for b in range(batch) for s in range(steps_n)], axis=0
+    )
     squares = jnp.sum(floated * floated, axis=1, keepdims=True)
     squares = jnp.broadcast_to(squares, (floated.shape[0], dim))
-    normed = (floated * gain_ref[...].astype(f32)).astype(bf16)
+    normed = (floated * gain_ref[...].astype(f32).reshape(1, width_local)).astype(bf16)
 
     table = table_ref[...]
     page_id = lax.broadcasted_iota(jnp.int32, (pages, table.shape[1]), 0) + me * pages
@@ -326,6 +330,11 @@
     for row, value in enumerate((owner_of, base_of, length_of, window_of)):
         info[row] = jnp.broadcast_to(value, (pages, dim)).astype(jnp.int32)
 
+    @pl.loop(0, pages)
+    def _(p):
+        found = jnp.sum(jnp.where(table[1:2, :] == me * pages + p, 1, 0))
+        owners[p] = jnp.minimum(found, batch - 1)
+
     wk_copy.wait()
     wv_copy.wait()
     pl.semaphore_wait(barrier, n - 1)
@@ -383,14 +392,25 @@
         spread(source(i))
 
     q_rows = queries.shape[1]
+    per_head = q_rows // kv_heads
+    groups = dim // per_head
+    part = page_len // groups
     for b in range(batch):
-        queries_t[b] = queries[b].T.astype(bf16)
+        turned = queries[b].T
+        for i in range(groups):
+            queries_t[b, i] = jnp.concatenate(
+                [
+                    pltpu.roll(turned[:, :dim], per_head * i, 1),
+                    pltpu.roll(turned[:, dim:], per_head * i, 1),
+                ],
+                axis=1,
+            ).astype(bf16)
 
     sub = lax.broadcasted_iota(jnp.int32, (kv_heads, dim), 0)
     lane = lax.broadcasted_iota(jnp.int32, (kv_heads, dim), 1)
-    per_head = q_rows // kv_heads
     lower = sub < kv_heads // 2
-    own_lane = (lane // per_head) == lax.rem(sub, kv_heads // 2)
+    group = lax.rem(lane // per_head - lax.rem(sub, groups) + groups, groups)
+    own_lane = group == 0
     full_head = jnp.zeros((kv_heads, dim), jnp.int32)
     for k in range(kv_heads):
         full_head = jnp.where(sub == k, retrieval_ref[k], full_head)
@@ -399,30 +419,43 @@
     @pl.loop(0, pages)
     def _(p):
         keys_copy(p).wait()
-        owner = info[0, pl.ds(p, 1), :]
-        base = info[1, pl.ds(p, 1), :]
-        until = jnp.where(own_lane, info[2, pl.ds(p, 1), :], 0) - base
+        base = info[1, pl.ds(p, 1), :] + part * group
+        until = info[2, pl.ds(p, 1), :] - base
         since = jnp.where(full_head, 0, info[3, pl.ds(p, 1), :]) - base
-        sinks = SINKS - jnp.broadcast_to(base, (kv_heads, dim))
-        wide_owner = jnp.concatenate([owner, owner], axis=1)
-        query = jnp.where(
-            wide_owner == 1, queries_t[1].astype(f32), queries_t[0].astype(f32)
-        ).astype(bf16)
-        scores = jnp.dot(keys_v[p], query, preferred_element_type=f32)
-        scores = scores.reshape(page_len, kv_heads, q_rows)
-        merged = jnp.where(lower[None], scores[:, :, :dim], scores[:, :, dim:]) * scale
-        token = lax.broadcasted_iota(jnp.int32, (page_len, kv_heads, dim), 0)
+        sinks = SINKS - base
+        merged = None
+        for i in range(groups):
+            rows = pl.ds(i * part * kv_heads, part * kv_heads)
+            scores = jnp.dot(keys_v[p, rows, :], queries_t[owners[p], i], preferred_element_type=f32)
+            scores = scores.reshape(part, kv_heads, q_rows)
+            scores = jnp.where(lower[None], scores[:, :, :dim], scores[:, :, dim:])
+            merged = scores if i == 0 else jnp.where((group == i)[None], scores, merged)
+        token = lax.broadcasted_iota(jnp.int32, (part, kv_heads, dim), 0)
         visible = (token < until[None]) & ((token >= since[None]) | (token < sinks[None]))
-        masked = jnp.where(visible, merged, very_low)
+        masked = jnp.where(visible, merged * scale, very_low)
         highest = jnp.max(masked, axis=0)
+        for shift in range(groups.bit_length() - 1):
+            highest = jnp.maximum(highest, pltpu.roll(highest, per_head << shift, 1))
         weights = jnp.where(visible, jnp.exp(masked - highest[None]), 0.0)
+        total = jnp.sum(weights, axis=0)
+        for shift in range(groups.bit_length() - 1):
+            total = total + pltpu.roll(total, per_head << shift, 1)
         page_max[p] = highest
-        page_total[p] = jnp.sum(weights, axis=0)
-        wide = jnp.concatenate(
-            [jnp.where(lower[None], weights, 0.0), jnp.where(lower[None], 0.0, weights)], axis=2
+        page_total[p] = total
+        wide = []
+        for i in range(groups):
+            turned = weights if i == 0 else pltpu.roll(weights, dim - per_head * i, 2)
+            both = jnp.concatenate(
+                [
+                    jnp.where((own_lane & lower)[None], turned, 0.0),
+                    jnp.where((own_lane & ~lower)[None], turned, 0.0),
+                ],
+                axis=2,
+            )
+            wide.append(both.reshape(part * kv_heads, q_rows).astype(bf16))
+        page_sum[p] = jnp.dot(
+            values_t[p], jnp.concatenate(wide, axis=0), preferred_element_type=f32
         )
-        wide = wide.reshape(page_len * kv_heads, q_rows).astype(bf16)
-        page_sum[p] = jnp.dot(values_t[p], wide, preferred_element_type=f32)
 
     def lanes_of(stat):
         kept = jnp.where(own_lane, stat, 0.0)
@@ -461,11 +494,17 @@
             wide_owner = jnp.concatenate([owner, owner], axis=1)
             acc += jnp.where(wide_owner == b, page_sum[p], 0.0)
         msg3[:, pl.ds(16 * b, 16), :] = acc.T.reshape(n, q_rows // n, dim)
-    stats = []
-    for b in range(batch):
-        for stat in (tops[b], totals[b]):
-            stats.append(jnp.broadcast_to(lanes_of(stat), (dim // 4, q_rows)))
-    msg3[:, pl.ds(32, 16), :] = jnp.concatenate(stats, axis=0).T.reshape(n, q_rows // n, dim)
+    stats = jnp.concatenate(
+        [lanes_of(tops[0]), lanes_of(tops[1]), lanes_of(totals[0]), lanes_of(totals[1])]
+        + [jnp.zeros((4, q_rows), f32)],
+        axis=0,
+    )
+    span = q_rows // n
+    for j in range(n):
+        at = j * span // dim * dim
+        moved = (dim - (j * span - at)) % dim
+        piece = stats[:, at : at + dim]
+        msg3[j, pl.ds(32, 8), :] = piece if moved == 0 else pltpu.roll(piece, moved, 1)
 
     @pl.loop(1, n)
     def _(i):
@@ -474,54 +513,53 @@
     recv3[me] = msg3[me]
 
     mine = pl.ds(pl.multiple_of(me * 16, 8), 16)
-    own_query = jnp.concatenate([queries[b, mine, :] for b in range(batch)], axis=0)
     head = me // 2
     new_key = gath[head, :, pl.ds(share, dim)]
     new_value = gath[kv_heads + head, :, pl.ds(share, dim)]
-    fresh = (
-        lax.dot_general(
-            own_query, new_key, (((1,), (1,)), ((), ())), preferred_element_type=f32
+    row = lax.broadcasted_iota(jnp.int32, (8, dim), 0)
+    col = lax.broadcasted_iota(jnp.int32, (8, dim), 1)
+    fresh_max = jnp.full((8, dim), very_low, f32)
+    fresh_total = jnp.zeros((8, dim), f32)
+    fresh_sum = []
+    for b in range(batch):
+        own_query = jnp.concatenate([queries[b, mine, :]] * (dim // 16), axis=0)
+        fresh = lax.dot_general(
+            new_key, own_query, (((1,), (1,)), ((), ())), preferred_element_type=f32
         )
-        * scale
-    )
-    row = lax.broadcasted_iota(jnp.int32, fresh.shape, 0)
-    col = lax.broadcasted_iota(jnp.int32, fresh.shape, 1)
-    causal = (row // 16 == col // steps_n) & (lax.rem(row, steps_n) >= lax.rem(col, steps_n))
-    fresh = jnp.where(causal, fresh, very_low)
-    fresh_max = jnp.max(fresh, axis=1, keepdims=True)
-    fresh_weights = jnp.where(causal, jnp.exp(fresh - fresh_max), 0.0)
-    fresh_total = jnp.sum(fresh_weights, axis=1, keepdims=True)
-    fresh_sum = jnp.dot(
-        fresh_weights.astype(bf16).astype(f32), new_value, preferred_element_type=f32
-    )
+        causal = (row // steps_n == b) & (lax.rem(row, steps_n) <= lax.rem(col, steps_n))
+        fresh = jnp.where(causal, fresh * scale, very_low)
+        highest = jnp.max(fresh, axis=0, keepdims=True)
+        weights = jnp.where(causal, jnp.exp(fresh - highest), 0.0)
+        fresh_max = jnp.where(row == b, highest, fresh_max)
+        fresh_total = jnp.where(row == b, jnp.sum(weights, axis=0, keepdims=True), fresh_total)
+        fresh_sum.append(
+            lax.dot_general(
+                weights.astype(bf16).astype(f32),
+                new_value,
+                (((0,), (0,)), ((), ())),
+                preferred_element_type=f32,
+            )[:16]
+        )
 
     @pl.loop(1, n)
     def _(i):
         remote(2, i, msg3.at[peer(i)], recv3.at[source(i)]).wait_recv()
 
-    top = lax.fori_loop(
-        0,
-        n,
-        lambda j, top: jnp.maximum(top, recv3[j, pl.ds(32, 16), :]),
-        jnp.full((16, dim), very_low, f32),
-    )
+    parts = recv3[:, pl.ds(32, 8), :]
+    top = jnp.maximum(jnp.max(parts, axis=0), fresh_max)
+    factor = jnp.exp(parts - top[None])
+    fresh_factor = jnp.exp(fresh_max - top)
+    total = jnp.sum(factor * pltpu.roll(parts, 8 - batch, 1), axis=0) + fresh_factor * fresh_total
+    total = jnp.where(row < batch, total, 1.0)
+    factor = factor / total[None]
+    fresh_factor = pltpu.roll(fresh_factor / total, 4, 0)
+    factor = jnp.where((row < 4)[None], factor, fresh_factor[None]).reshape(n * 8, dim).T[:16]
     attended = []
     for b in range(batch):
-        rows = slice(16 * b, 16 * b + 16)
-        highest = jnp.maximum(top[:, 64 * b : 64 * b + 1], fresh_max[rows])
-        factor = jnp.exp(fresh_max[rows] - highest)
-        total = fresh_total[rows] * factor
-        acc = fresh_sum[rows] * factor
-
-        def merge_turn(j, state, b=b, highest=highest):
-            total, acc = state
-            stat = recv3[j, pl.ds(32, 16), :]
-            factor = jnp.exp(stat[:, 64 * b : 64 * b + 1] - highest)
-            total = total + stat[:, 64 * b + 32 : 64 * b + 33] * factor
-            return total, acc + recv3[j, pl.ds(16 * b, 16), :] * factor
-
-        total, acc = lax.fori_loop(0, n, merge_turn, (total, acc))
-        attended.append(acc / total)
+        acc = fresh_sum[b] * factor[:, 4 + b : 5 + b]
+        for j in range(n):
+            acc += recv3[j, pl.ds(16 * b, 16), :] * factor[:, 8 * j + b : 8 * j + b + 1]
+        attended.append(acc)
     first = swap_halves(attended[0][:8], attended[1][:8])
     second = swap_halves(attended[0][8:], attended[1][8:])
     attended = jnp.concatenate(first + second, axis=1).astype(bf16)
@@ -535,7 +573,11 @@
         msg4[i] = project_out(i)
         remote(3, i, msg4.at[i], recv4.at[me]).start()
 
-    out_ref[...] = add_up(3, msg4, recv4, project_out(0))
+    result = add_up(3, msg4, recv4, project_out(0))
+    for s in range(steps_n):
+        out_ref[s] = jnp.concatenate(
+            [result[b * steps_n + s : b * steps_n + s + 1] for b in range(batch)], axis=0
+        ).astype(out_ref.dtype)
 
     @pl.loop(1, n)
     def _(i):
@@ -588,7 +630,7 @@
     dma = pltpu.SemaphoreType.DMA
     out = pl.pallas_call(
         functools.partial(fused, n, steps_n, batch, kv_heads, page_len),
-        out_shape=jax.ShapeDtypeStruct((rows, w_output.shape[1] // n), f32),
+        out_shape=jax.ShapeDtypeStruct((steps_n, batch, w_output.shape[1] // n), bf16),
         in_specs=[smem] * 3 + [vmem] * 3 + [hbm] * 6,
         out_specs=vmem,
         scratch_shapes=[
@@ -602,13 +644,14 @@
             pltpu.VMEM((n, rows, share + 2 * dim), f32),
             pltpu.VMEM((n, rows, share + dim), f32),
             pltpu.VMEM((batch, q_rows, dim), f32),
-            pltpu.VMEM((batch, dim, q_rows), bf16),
+            pltpu.VMEM((batch, dim // (q_rows // kv_heads), dim, q_rows), bf16),
             pltpu.VMEM((4, pages, dim), jnp.int32),
+            pltpu.SMEM((pages,), jnp.int32),
             pltpu.VMEM((pages, kv_heads, dim), f32),
             pltpu.VMEM((pages, kv_heads, dim), f32),
             pltpu.VMEM((pages, dim, q_rows), f32),
-            pltpu.VMEM((n, 48, dim), f32),
-            pltpu.VMEM((n, 48, dim), f32),
+            pltpu.VMEM((n, 40, dim), f32),
+            pltpu.VMEM((n, 40, dim), f32),
             pltpu.VMEM((n, rows, share), f32),
             pltpu.VMEM((n, rows, share), f32),
             dma((n,)),
@@ -626,8 +669,8 @@
         retrieval,
         lengths,
         window_start,
-        jnp.transpose(hidden, (1, 0, 2)).reshape(rows, width_local),
-        norm_gain.reshape(1, width_local),
+        hidden,
+        norm_gain,
         page_table,
         w_query,
         w_key,
@@ -636,8 +679,7 @@
         key_cache.reshape(pages, page_len * kv_heads, dim),
         value_cache.reshape(pages, page_len * kv_heads, dim),
     )
-    out = out.reshape(batch, steps_n, out.shape[1])
-    return jnp.transpose(out, (1, 0, 2)).astype(bf16)
+    return out
 
 
 def solution(mesh):

time: 66 us -> 60.1 us (0.911)
  Pallas kernels: 61.7 us -> 58.5 us
  local copies, waits for them, and re-layouts: 3.2 us -> 1.3 us
  other arithmetic: 0.72 us -> 0 us
    pallas_call x1, Pallas kernels: 61.7 us -> 58.5 us  [local(): pl.pallas_call(functools.partial(fused, n, steps_n, batch, kv_heads, page...]
    reshape x2 -> x0, local copies, waits for them, and re-layouts: 1.88 us -> none  [the longest x1 1.27 us: local(): norm_gain.reshape(1, width_local)]
    unnamed x0 -> x1, local copies, waits for them, and re-layouts: none -> 1.3 us
    convert_element_type x1 -> x0, other arithmetic: 0.72 us -> none  [local(): return jnp.transpose(out, (1, 0, 2)).astype(bf16)]
    transpose x1 -> x0, local copies, waits for them, and re-layouts: 0.7 us -> none  [local(): jnp.transpose(hidden, (1, 0, 2)).reshape(rows, width_local)]
where the time goes in v2:
time: 60.1 us; the launch traced here: 59.8 us
  Pallas kernels  58.5 us (97%)
  local copies, waits for them, and re-layouts  1.3 us (2%)
    pallas_call x1, Pallas kernels, local(): pl.pallas_call(functools.partial(fused, n, steps_n, batch, kv_heads, page...  58.5 us
    unnamed x1, local copies, waits for them, and re-layouts  1.3 us

profile of v2, /device:TPU:0, one launch (start us, length us, event | category | flops | bytes accessed | tf_op | source)
XLA Modules:
  0.0 59.8 jit_solution(2734681270860444098)
XLA Ops:
  0.0 58.5 %shard_map.118 = bf16[4,2,512]{2,1,0:T(2,128)(2,1)} custom-call(s32[8]{0:T(128)} %retrieval_ref.1, s32[2]{0:T(128)} %lengths_ref.1, s32[2]{0:T(128)} %window_ref.1, bf16[4,2,512]{2,1,0:T(2,128)(2,1)} %hidden_ref.1, bf16[512]{0:T(512)(128)(2,1)} %gain_ref.1, s32[2,128]{1,0:T(2,128)} %table_ref.1, bf16[512,8192]{1,0:T(8,128)(2,1)} %wq_hbm.1, ...), custom_call_target="tpu_custom_call" | custom-call | tf_op jit(solution)/shard_map/pallas_call | solution.py:631
  58.5 1.3 %copy.14 = bf16[4,2,512]{2,1,0:T(2,128)(2,1)} copy(bf16[4,2,512]{2,1,0:T(2,128)(2,1)} %shard_map.118) | data formatting | bytes 16384

commit v3 on v2

--- a/solution.py
+++ b/solution.py
@@ -243,6 +243,7 @@
     dim = 128
     width_local = hidden_ref.shape[2]
     scale = dim ** (-0.5)
+    half = n // 2
 
     def peer(i):
         return lax.rem(me + i, n)
@@ -250,12 +251,21 @@
     def source(i):
         return lax.rem(me + n - i, n)
 
+    twin = me + 1 - 2 * lax.rem(me, 2)
+
+    def twin_peer(i):
+        return lax.rem(twin + i, n)
+
+    def target(k):
+        odd = lax.rem(k, 2)
+        return lax.rem(me + odd * (twin - me) + k - odd, n)
+
     def wq_copy(i):
-        cols = pl.ds(pl.multiple_of(peer(i) * share, 128), share)
+        cols = pl.ds(pl.multiple_of(target(i) * share, 128), share)
         return pltpu.make_async_copy(wq_hbm.at[:, cols], wq_v.at[i], wq_sem.at[i])
 
     def wo_copy(i):
-        cols = pl.ds(pl.multiple_of(peer(i) * share, 128), share)
+        cols = pl.ds(pl.multiple_of(target(i) * share, 128), share)
         return pltpu.make_async_copy(wo_hbm.at[:, cols], wo_v.at[i], wo_sem.at[i])
 
     kv_width = kv_heads * dim
@@ -268,13 +278,13 @@
     def values_copy(p):
         return pltpu.make_async_copy(values_hbm.at[p], values_v.at[p], values_sem.at[p])
 
-    def remote(phase, i, from_ref, to_ref):
+    def remote(phase, i, from_ref, to_ref, device):
         return pltpu.make_async_remote_copy(
             src_ref=from_ref,
             dst_ref=to_ref,
             send_sem=send_sem.at[phase, i],
             recv_sem=recv_sem.at[phase, i],
-            device_id={"ctx": peer(i)},
+            device_id={"ctx": device},
             device_id_type=pl.DeviceIdType.MESH,
         )
 
@@ -289,9 +299,13 @@
     wk_copy.start()
     wv_copy.start()
 
-    @pl.loop(1, n + 1)
-    def _(i):
-        wq_copy(lax.rem(i, n)).start()
+    @pl.loop(1, half + 1)
+    def _(h):
+        wq_copy(lax.rem(2 * h, n) + 1).start()
+
+    @pl.loop(1, half + 1)
+    def _(h):
+        wq_copy(lax.rem(2 * h, n)).start()
 
     @pl.loop(0, pages)
     def _(p):
@@ -301,9 +315,13 @@
     def _(p):
         keys_copy(p).start()
 
-    @pl.loop(1, n + 1)
-    def _(i):
-        wo_copy(lax.rem(i, n)).start()
+    @pl.loop(1, half + 1)
+    def _(h):
+        wo_copy(lax.rem(2 * h, n) + 1).start()
+
+    @pl.loop(1, half + 1)
+    def _(h):
+        wo_copy(lax.rem(2 * h, n)).start()
 
     loaded = hidden_ref[...].astype(f32)
     floated = jnp.concatenate(
@@ -341,39 +359,56 @@
 
     def project(i, to_ref):
         wq_copy(i).wait()
-        cols = pl.ds(pl.multiple_of(peer(i) * dim, 128), dim)
+        cols = pl.ds(pl.multiple_of(target(i) * dim, 128), dim)
         to_ref[:, pl.ds(0, share)] = jnp.dot(normed, wq_v[i], preferred_element_type=f32)
         to_ref[:, pl.ds(share, dim)] = jnp.dot(normed, wkv_v[:, cols], preferred_element_type=f32)
         to_ref[:, pl.ds(share + dim, dim)] = squares
 
-    @pl.loop(1, n)
-    def _(i):
-        project(i, msg1.at[i])
-        remote(0, i, msg1.at[i], recv1.at[me]).start()
-
-    project(0, recv1.at[me])
+    def scatter(phase, fill, msg, recv):
+        @pl.loop(1, half + 1)
+        def _(h):
+            e = lax.rem(2 * h, n)
+            fill(e + 1, msg.at[e + 1])
+            remote(phase, e + 1, msg.at[e + 1], recv.at[peer(e)], twin).start()
+
+        @pl.loop(1, half)
+        def _(h):
+            e = 2 * h
+            fill(e, msg.at[e])
+            remote(phase, e + 1, msg.at[e + 1], recv.at[twin_peer(e)], twin).wait_recv()
+            msg[e] = msg[e] + recv[twin_peer(e)]
+            remote(phase, e, msg.at[e], recv.at[me], peer(e)).start()
+
+        fill(0, msg.at[0])
+
+    scatter(0, project, msg1, recv1)
 
     @pl.loop(0, pages)
     def _(p):
         values_copy(p).wait()
         values_t[p] = values_v[p].T
 
-    def add_up(phase, msg, recv, acc):
-        def turn(i, acc):
-            remote(phase, i, msg.at[i], recv.at[source(i)]).wait_recv()
-            return acc + recv[source(i)]
-
-        return lax.fori_loop(1, n, turn, acc)
-
-    summed = add_up(0, msg1, recv1, recv1[me])
+    def add_up(phase, msg, recv):
+        remote(phase, 1, msg.at[1], recv.at[twin], twin).wait_recv()
+
+        def turn(h, acc):
+            e = 2 * h
+            remote(phase, e, msg.at[e], recv.at[source(e)], peer(e)).wait_recv()
+            return acc + recv[source(e)]
+
+        return lax.fori_loop(1, half, turn, msg[0] + recv[twin])
+
+    summed = add_up(0, msg1, recv1)
     inv_rms = lax.rsqrt(summed[:, share + dim :] / (width_local * n) + epsilon)
     for c in range((share + dim) // dim):
         piece = summed[:, c * dim : (c + 1) * dim] * inv_rms
         gath[me, :, pl.ds(c * dim, dim)] = piece.astype(bf16).astype(f32)
 
-    @pl.loop(1, n)
-    def _(i):
-        remote(1, i, gath.at[me], gath.at[me]).start()
+    @pl.loop(1, half)
+    def _(h):
+        remote(1, 2 * h, gath.at[me], gath.at[me], peer(2 * h)).start()
+
+    remote(1, 1, gath.at[me], gath.at[me], twin).start()
 
     def spread(j):
         rows = pl.multiple_of(j * 2 * steps_n * batch, 8)
@@ -386,10 +421,20 @@
 
     spread(me)
 
-    @pl.loop(1, n)
-    def _(i):
-        remote(1, i, gath.at[me], gath.at[source(i)]).wait_recv()
-        spread(source(i))
+    @pl.loop(1, half)
+    def _(h):
+        e = 2 * h
+        block = gath.at[source(e)]
+        remote(1, e, gath.at[me], block, peer(e)).wait_recv()
+        remote(1, e + 1, block, block, twin).start()
+        spread(source(e))
+
+    @pl.loop(0, half)
+    def _(h):
+        e = 2 * h
+        origin = lax.rem(twin + n - e, n)
+        remote(1, e + 1, gath.at[me], gath.at[origin], twin).wait_recv()
+        spread(origin)
 
     q_rows = queries.shape[1]
     per_head = q_rows // kv_heads
@@ -416,21 +461,25 @@
         full_head = jnp.where(sub == k, retrieval_ref[k], full_head)
     full_head = full_head == 1
 
-    @pl.loop(0, pages)
-    def _(p):
-        keys_copy(p).wait()
+    own_low, own_high = own_lane & lower, own_lane & ~lower
+    token = lax.broadcasted_iota(jnp.int32, (part, kv_heads, dim), 0)
+
+    def page_scores(p):
+        query = owners[p]
+        merged = None
+        for i in range(groups):
+            rows = pl.ds(i * part * kv_heads, part * kv_heads)
+            scores = jnp.dot(keys_v[p, rows, :], queries_t[query, i], preferred_element_type=f32)
+            scores = scores.reshape(part, kv_heads, q_rows)
+            scores = jnp.where(lower[None], scores[:, :, :dim], scores[:, :, dim:])
+            merged = scores if i == 0 else jnp.where((group == i)[None], scores, merged)
+        return merged
+
+    def page_weights(p, merged):
         base = info[1, pl.ds(p, 1), :] + part * group
         until = info[2, pl.ds(p, 1), :] - base
         since = jnp.where(full_head, 0, info[3, pl.ds(p, 1), :]) - base
         sinks = SINKS - base
-        merged = None
-        for i in range(groups):
-            rows = pl.ds(i * part * kv_heads, part * kv_heads)
-            scores = jnp.dot(keys_v[p, rows, :], queries_t[owners[p], i], preferred_element_type=f32)
-            scores = scores.reshape(part, kv_heads, q_rows)
-            scores = jnp.where(lower[None], scores[:, :, :dim], scores[:, :, dim:])
-            merged = scores if i == 0 else jnp.where((group == i)[None], scores, merged)
-        token = lax.broadcasted_iota(jnp.int32, (part, kv_heads, dim), 0)
         visible = (token < until[None]) & ((token >= since[None]) | (token < sinks[None]))
         masked = jnp.where(visible, merged * scale, very_low)
         highest = jnp.max(masked, axis=0)
@@ -440,22 +489,38 @@
         total = jnp.sum(weights, axis=0)
         for shift in range(groups.bit_length() - 1):
             total = total + pltpu.roll(total, per_head << shift, 1)
-        page_max[p] = highest
-        page_total[p] = total
         wide = []
         for i in range(groups):
             turned = weights if i == 0 else pltpu.roll(weights, dim - per_head * i, 2)
             both = jnp.concatenate(
                 [
-                    jnp.where((own_lane & lower)[None], turned, 0.0),
-                    jnp.where((own_lane & ~lower)[None], turned, 0.0),
+                    jnp.where(own_low[None], turned, 0.0),
+                    jnp.where(own_high[None], turned, 0.0),
                 ],
                 axis=2,
             )
             wide.append(both.reshape(part * kv_heads, q_rows).astype(bf16))
-        page_sum[p] = jnp.dot(
-            values_t[p], jnp.concatenate(wide, axis=0), preferred_element_type=f32
-        )
+        return highest, total, jnp.concatenate(wide, axis=0)
+
+    at_once = 4
+
+    @pl.loop(0, pages)
+    def _(p):
+        keys_copy(p).wait()
+
+    @pl.loop(0, pages // at_once)
+    def _(g):
+        block = [g * at_once + u for u in range(at_once)]
+        scored = [page_scores(p) for p in block]
+        weighed = [page_weights(p, merged) for p, merged in zip(block, scored)]
+        summed = [
+            jnp.dot(values_t[p], wide, preferred_element_type=f32)
+            for p, (_, _, wide) in zip(block, weighed)
+        ]
+        for p, (highest, total, _), page in zip(block, weighed, summed):
+            page_max[p] = highest
+            page_total[p] = total
+            page_sum[p] = page
 
     def lanes_of(stat):
         kept = jnp.where(own_lane, stat, 0.0)
@@ -508,7 +573,7 @@
 
     @pl.loop(1, n)
     def _(i):
-        remote(2, i, msg3.at[peer(i)], recv3.at[me]).start()
+        remote(2, i, msg3.at[peer(i)], recv3.at[me], peer(i)).start()
 
     recv3[me] = msg3[me]
 
@@ -543,7 +608,7 @@
 
     @pl.loop(1, n)
     def _(i):
-        remote(2, i, msg3.at[peer(i)], recv3.at[source(i)]).wait_recv()
+        remote(2, i, msg3.at[peer(i)], recv3.at[source(i)], peer(i)).wait_recv()
 
     parts = recv3[:, pl.ds(32, 8), :]
     top = jnp.maximum(jnp.max(parts, axis=0), fresh_max)
@@ -564,16 +629,12 @@
     second = swap_halves(attended[0][8:], attended[1][8:])
     attended = jnp.concatenate(first + second, axis=1).astype(bf16)
 
-    def project_out(i):
+    def project_out(i, to_ref):
         wo_copy(i).wait()
-        return jnp.dot(attended, wo_v[i], preferred_element_type=f32)
-
-    @pl.loop(1, n)
-    def _(i):
-        msg4[i] = project_out(i)
-        remote(3, i, msg4.at[i], recv4.at[me]).start()
-
-    result = add_up(3, msg4, recv4, project_out(0))
+        to_ref[...] = jnp.dot(attended, wo_v[i], preferred_element_type=f32)
+
+    scatter(3, project_out, msg4, recv4)
+    result = add_up(3, msg4, recv4)
     for s in range(steps_n):
         out_ref[s] = jnp.concatenate(
             [result[b * steps_n + s : b * steps_n + s + 1] for b in range(batch)], axis=0
@@ -581,10 +642,10 @@
 
     @pl.loop(1, n)
     def _(i):
-        remote(0, i, msg1.at[i], recv1.at[me]).wait_send()
-        remote(1, i, gath.at[me], gath.at[me]).wait_send()
-        remote(2, i, msg3.at[peer(i)], recv3.at[me]).wait_send()
-        remote(3, i, msg4.at[i], recv4.at[me]).wait_send()
+        remote(0, i, msg1.at[i], recv1.at[me], peer(i)).wait_send()
+        remote(1, i, gath.at[me], gath.at[me], peer(i)).wait_send()
+        remote(2, i, msg3.at[peer(i)], recv3.at[me], peer(i)).wait_send()
+        remote(3, i, msg4.at[i], recv4.at[me], peer(i)).wait_send()
 
 
 def local(
@@ -608,7 +669,7 @@
     share = query_width // n
     rows = steps_n * batch
     q_rows = query_width // dim * steps_n
-    if (n, share, rows, batch, kv_heads, dim) != (2 * kv_heads, 4 * dim, 8, 2, 8, 128):
+    if pages % 4 or (n, share, rows, batch, kv_heads, dim) != (2 * kv_heads, 4 * dim, 8, 2, 8, 128):
         return local_small(
             hidden,
             norm_gain,

time: 60.1 us -> 46.8 us (0.78)
  Pallas kernels: 58.5 us -> 45.3 us
    pallas_call x1, Pallas kernels: 58.5 us -> 45.3 us  [local(): pl.pallas_call(functools.partial(fused, n, steps_n, batch, kv_heads, page...]
where the time goes in v3:
time: 46.8 us; the launch traced here: 46.6 us
  Pallas kernels  45.3 us (97%)
  local copies, waits for them, and re-layouts  1.3 us (3%)
    pallas_call x1, Pallas kernels, local(): pl.pallas_call(functools.partial(fused, n, steps_n, batch, kv_heads, page...  45.3 us
    unnamed x1, local copies, waits for them, and re-layouts  1.3 us

profile of v3, /device:TPU:0, one launch (start us, length us, event | category | flops | bytes accessed | tf_op | source)
XLA Modules:
  0.0 46.6 jit_solution(6159191997235515372)
XLA Ops:
  0.0 45.3 %shard_map.118 = bf16[4,2,512]{2,1,0:T(2,128)(2,1)} custom-call(s32[8]{0:T(128)} %retrieval_ref.1, s32[2]{0:T(128)} %lengths_ref.1, s32[2]{0:T(128)} %window_ref.1, bf16[4,2,512]{2,1,0:T(2,128)(2,1)} %hidden_ref.1, bf16[512]{0:T(512)(128)(2,1)} %gain_ref.1, s32[2,128]{1,0:T(2,128)} %table_ref.1, bf16[512,8192]{1,0:T(8,128)(2,1)} %wq_hbm.1, ...), custom_call_target="tpu_custom_call" | custom-call | tf_op jit(solution)/shard_map/pallas_call | solution.py:692
  45.3 1.3 %copy.14 = bf16[4,2,512]{2,1,0:T(2,128)(2,1)} copy(bf16[4,2,512]{2,1,0:T(2,128)(2,1)} %shard_map.118) | data formatting | bytes 16384

commit v4 on v3

--- a/solution.py
+++ b/solution.py
@@ -502,7 +502,7 @@
             wide.append(both.reshape(part * kv_heads, q_rows).astype(bf16))
         return highest, total, jnp.concatenate(wide, axis=0)
 
-    at_once = 4
+    at_once = 8
 
     @pl.loop(0, pages)
     def _(p):
@@ -669,7 +669,7 @@
     share = query_width // n
     rows = steps_n * batch
     q_rows = query_width // dim * steps_n
-    if pages % 4 or (n, share, rows, batch, kv_heads, dim) != (2 * kv_heads, 4 * dim, 8, 2, 8, 128):
+    if pages % 8 or (n, share, rows, batch, kv_heads, dim) != (2 * kv_heads, 4 * dim, 8, 2, 8, 128):
         return local_small(
             hidden,
             norm_gain,

time: 46.8 us -> 45.8 us (0.979)
  Pallas kernels: 45.3 us -> 44.2 us
    pallas_call x1, Pallas kernels: 45.3 us -> 44.2 us  [local(): pl.pallas_call(functools.partial(fused, n, steps_n, batch, kv_heads, page...]
where the time goes in v4:
time: 45.8 us; the launch traced here: 45.5 us
  Pallas kernels  44.2 us (97%)
  local copies, waits for them, and re-layouts  1.3 us (3%)
    pallas_call x1, Pallas kernels, local(): pl.pallas_call(functools.partial(fused, n, steps_n, batch, kv_heads, page...  44.2 us
    unnamed x1, local copies, waits for them, and re-layouts  1.3 us

profile of v4, /device:TPU:0, one launch (start us, length us, event | category | flops | bytes accessed | tf_op | source)
XLA Modules:
  0.0 45.5 jit_solution(5144707229068637410)
XLA Ops:
  0.0 44.2 %shard_map.118 = bf16[4,2,512]{2,1,0:T(2,128)(2,1)} custom-call(s32[8]{0:T(128)} %retrieval_ref.1, s32[2]{0:T(128)} %lengths_ref.1, s32[2]{0:T(128)} %window_ref.1, bf16[4,2,512]{2,1,0:T(2,128)(2,1)} %hidden_ref.1, bf16[512]{0:T(512)(128)(2,1)} %gain_ref.1, s32[2,128]{1,0:T(2,128)} %table_ref.1, bf16[512,8192]{1,0:T(8,128)(2,1)} %wq_hbm.1, ...), custom_call_target="tpu_custom_call" | custom-call | tf_op jit(solution)/shard_map/pallas_call | solution.py:692
  44.2 1.3 %copy.14 = bf16[4,2,512]{2,1,0:T(2,128)(2,1)} copy(bf16[4,2,512]{2,1,0:T(2,128)(2,1)} %shard_map.118) | data formatting | bytes 16384
